TPU v7x, 32 devices: a whole 2x2x4 slice. The times are simulated.
32 devices in a mesh: groups: 2 (over y), rows: 4 (over z), cols: 2 (over x), chan: 2 (over core).
Axes of the slice: x: 2, y: 2, z: 4, core: 2. Of those that a mesh axis runs over, the one named last changes fastest.
Arguments:
- patches: bfloat16 [128, 16, 1024], P(('groups', 'rows'), 'cols', 'chan'), parts along dimension 0, may hold values from -6 to 6
- steps: float32 [128, 16, 1024], P(('groups', 'rows'), 'cols', 'chan'), parts along dimension 0, may hold values from 0.1 to 1
- decay_codes: int32 [128, 16], P(('groups', 'rows'), 'cols'), parts along dimension 0, may hold values from 0 to 15
- tissue_mask: int32 [128, 16], P(('groups', 'rows'), 'cols'), parts along dimension 0, may hold values 0 or 1
- decay_rates: float32 [16, 1024], P(None, 'chan'), may hold values from 0.002 to 4
- input_map: float32 [128, 16, 16], P(('groups', 'rows'), 'cols'), parts along dimension 0, may hold values from -1.5 to 1.5
- output_map: float32 [128, 16, 16], P(('groups', 'rows'), 'cols'), parts along dimension 0, may hold values from -1.5 to 1.5
- out_grad: bfloat16 [128, 16, 1024], P(('groups', 'rows'), 'cols', 'chan'), parts along dimension 0, may hold values from -0.59765625 to 0.59765625
Outputs:
- patches_grad: bfloat16 [128, 16, 1024], P(('groups', 'rows'), 'cols', 'chan'), parts along dimension 0
- steps_grad: float32 [128, 16, 1024], P(('groups', 'rows'), 'cols', 'chan'), parts along dimension 0
- input_map_grad: float32 [128, 16, 16], P(('groups', 'rows'), 'cols'), parts along dimension 0
- output_map_grad: float32 [128, 16, 16], P(('groups', 'rows'), 'cols'), parts along dimension 0
There are 2 independent parts, one for each index of `groups`. A program takes and returns all parts, laid end to end along the dimension named above; an argument that names none is the same for every part. Nothing has to cross between parts.
Inputs may be any that keep to these rules, and one draw needn't show every extreme that they name: `decay_codes`: a decay code of each patch.
All inputs are finite; a program needn't handle non-finite values. No bound on the sum of `tissue_mask` on one device may be relied on, other than what follows from the above.
Results may differ from a plain program's by a relative error of at most 0.0014.
Values sent between devices are 32-bit elements; how exact they have to be, the bound alone decides.
No kernel may reach another device: no remote copies, remote signals or barrier semaphores. Data moves between devices by JAX's collectives and lax.ppermute only.
A program may use at most 128 MiB of HBM per device.

v0:
```python
import jax
import jax.numpy as jnp
from jax import lax
from jax.sharding import PartitionSpec as P

CODES = 16


def shifted(block, axis, distance):
    devices = range(lax.axis_size(axis))
    route = [(i - distance, i) for i in devices if i - distance in devices]
    return lax.ppermute(block, axis, route)


def relay_carry(factor, offset, sender, count):

    def advance(turn, carry):
        return sender(factor * carry + offset)

    return lax.fori_loop(0, count, advance, jnp.zeros_like(offset))


def local(patches, steps, decay_codes, tissue_mask, decay_rates, input_map, output_map, out_grad):
    prows = steps.shape[0]
    pcols = steps.shape[1]
    maskf = tissue_mask.astype(jnp.float32)
    levels = 0.7 + 0.25 * decay_codes.astype(jnp.float32) / (CODES - 1)
    keep = maskf * jnp.log(levels)
    xf = patches.astype(jnp.float32)
    gyf = out_grad.astype(jnp.float32)
    drive = maskf[:, :, None] * steps * xf
    log_step = keep[:, :, None] * steps
    row_expo = jnp.sum(log_step, axis=1)
    col_expo = jnp.sum(log_step, axis=0)
    row_factor = jnp.exp(row_expo[:, None, :] * decay_rates[None])
    col_factor = jnp.exp(col_expo[:, None, :] * decay_rates[None])
    row_zero = jnp.zeros(row_factor.shape, jnp.float32)
    col_zero = jnp.zeros(col_factor.shape, jnp.float32)

    def decay_of(kept, stepped):
        return jnp.exp(kept[:, None, None] * decay_rates[None] * stepped[:, None, :])

    def row_forward(carry, j):
        factor = decay_of(keep[:, j], steps[:, j])
        carry = factor * carry + input_map[:, j, :, None] * drive[:, j][:, None, :]
        return (carry, carry)

    def row_forward_last(carry, j):
        return (row_forward(carry, j)[0], None)

    row_offset, _ = lax.scan(row_forward_last, row_zero, jnp.arange(pcols))
    left_in = relay_carry(
        row_factor, row_offset, lambda value: shifted(value, "cols", 1), lax.axis_size("cols") - 1
    )
    _, row_state_t = lax.scan(row_forward, left_in, jnp.arange(pcols))

    def col_forward(carry, i):
        factor = decay_of(keep[i], steps[i])
        carry = factor * carry + row_state_t[:, i]
        return (carry, carry)

    def col_forward_last(carry, i):
        return (col_forward(carry, i)[0], None)

    col_offset, _ = lax.scan(col_forward_last, col_zero, jnp.arange(prows))
    top_in = relay_carry(
        col_factor, col_offset, lambda value: shifted(value, "rows", 1), lax.axis_size("rows") - 1
    )

    def col_forward_out(carry, i):
        carry, _ = col_forward(carry, i)
        return (carry, (carry, jnp.sum(gyf[i][:, None, :] * carry, axis=2)))

    _, (state, map_out) = lax.scan(col_forward_out, top_in, jnp.arange(prows))

    def col_backward(carry, i):
        factor = decay_of(keep[i], steps[i])
        cot = output_map[i][:, :, None] * gyf[i][:, None, :] + carry
        return (factor * cot, cot)

    def col_backward_last(carry, i):
        return (col_backward(carry, i)[0], None)

    up_offset, _ = lax.scan(col_backward_last, col_zero, jnp.arange(prows), reverse=True)
    bottom_in = relay_carry(
        col_factor, up_offset, lambda value: shifted(value, "rows", -1), lax.axis_size("rows") - 1
    )
    _, col_cot = lax.scan(col_backward, bottom_in, jnp.arange(prows), reverse=True)

    def row_backward_last(carry, j):
        factor = decay_of(keep[:, j], steps[:, j])
        return (factor * (col_cot[:, j] + carry), None)

    lead_offset, _ = lax.scan(row_backward_last, row_zero, jnp.arange(pcols), reverse=True)
    right_in = relay_carry(
        row_factor, lead_offset, lambda value: shifted(value, "cols", -1), lax.axis_size("cols") - 1
    )

    def row_backward(carry, j):
        kept = keep[:, j]
        stepped = steps[:, j]
        factor = decay_of(kept, stepped)
        col_here = col_cot[:, j]
        row_here = col_here + carry
        state_col = state[:, j]
        above = jnp.concatenate([top_in[j][None], state_col[:-1]], axis=0)
        left = jnp.where(j > 0, row_state_t[jnp.maximum(j - 1, 0)], left_in)
        decay_cot = factor * (col_here * above + row_here * left)
        drive_cot = jnp.sum(row_here * input_map[:, j, :, None], axis=1)
        masked = maskf[:, j][:, None]
        grad_x = (drive_cot * masked * stepped).astype(jnp.bfloat16)
        grad_s = drive_cot * masked * xf[:, j] + jnp.sum(
            decay_cot * kept[:, None, None] * decay_rates[None], axis=1
        )
        grad_in = jnp.sum(row_here * drive[:, j][:, None, :], axis=2)
        return (factor * row_here, (grad_x, grad_s, grad_in))

    _, (grad_x, grad_s, map_in) = lax.scan(row_backward, right_in, jnp.arange(pcols), reverse=True)
    patches_grad = jnp.moveaxis(grad_x, 0, 1)
    steps_grad = jnp.moveaxis(grad_s, 0, 1)
    map_in = jnp.moveaxis(map_in, 0, 1)
    input_grad, output_grad = lax.psum((map_in, map_out), "chan")
    return (patches_grad, steps_grad, input_grad, output_grad)


def solution(mesh):
    in_specs = (
        P(("groups", "rows"), "cols", "chan"),
        P(("groups", "rows"), "cols", "chan"),
        P(("groups", "rows"), "cols"),
        P(("groups", "rows"), "cols"),
        P(None, "chan"),
        P(("groups", "rows"), "cols", None),
        P(("groups", "rows"), "cols", None),
        P(("groups", "rows"), "cols", "chan"),
    )
    out_specs = (
        P(("groups", "rows"), "cols", "chan"),
        P(("groups", "rows"), "cols", "chan"),
        P(("groups", "rows"), "cols", None),
        P(("groups", "rows"), "cols", None),
    )
    return jax.shard_map(local, mesh=mesh, in_specs=in_specs, out_specs=out_specs, check_vma=False)
```

profile of v0, /device:TPU:0, one launch (start us, length us, event | category | flops | bytes accessed | tf_op | source)
XLA Modules:
  0.0 537.3 jit_solution(17045311224574142558)
XLA Ops:
  4.3 77.7 %while.151 = (s32[]{:T(128)}, f32[8,16,512]{2,1,0:T(8,128)S(1)}, s32[16]{0:T(128)S(1)}, f32[16,8]{1,0:T(8,128)S(1)}, f32[16,512]{1,0:T(8,128)}, /*index=5*/f32[1...) while((s32[]{:T(128)}, f32[8,16,512]{2,1,0:T(8,128)S(1)}, ...), condition=%wide.region_3.4_spmd.clone, body=%wide.region_2.3_spmd.clone.sunk | while | flops 393223 | bytes 657189 | solution.py:84
  82.1 31.6 %while.149 = (s32[]{:T(128)}, f32[8,16,512]{2,1,0:T(8,128)S(1)}, f32[8,16,512]{2,1,0:T(8,128)S(1)}, f32[16,512]{1,0:T(8,128)}, f32[8,512]{1,0:T(8,128)S(1)}, /*index=5*/s32[]{:T(128)}) while((s32[]{:T(128)}, f32[8,16,512]{2,1,0:T(8,128)S(1)}, f32[8,16,512]{2,1,0:T(8,128)S(1)}, f32[16,512]{1,0:T(8,128)}, f32[8,512]{1,0:T(8,128)S(1)}, ...), condition=%wide.region_5.6_spmd.clone, body=%wide.region_4.5_spmd.clone.sunk | while | flops 196610 | bytes 1884269 | solution.py:20
  83.0 1.3 collective-permute-start
  84.3 10.0 %collective-permute-done = f32[8,16,512]{2,1,0:T(8,128)S(1)} collective-permute-done((f32[8,16,512]{2,1,0:T(8,128)S(1)}, f32[8,16,512]{2,1,0:T(8,128)S(1)}, u32[]{:S(2)}, u32[]{:S(2)}) %collective-permute-start) | collective-permute-done | bytes 262176 | tf_op jit(solution)/shard_map/while/body/eval_jaxpr/ppermute | solution.py:12
  95.0 1.3 collective-permute-start
  96.3 8.1 %collective-permute-done = f32[8,16,512]{2,1,0:T(8,128)S(1)} collective-permute-done((f32[8,16,512]{2,1,0:T(8,128)S(1)}, f32[8,16,512]{2,1,0:T(8,128)S(1)}, u32[]{:S(2)}, u32[]{:S(2)}) %collective-permute-start) | collective-permute-done | bytes 262176 | tf_op jit(solution)/shard_map/while/body/eval_jaxpr/ppermute | solution.py:12
  105.2 1.3 collective-permute-start
  106.5 7.2 %collective-permute-done = f32[8,16,512]{2,1,0:T(8,128)S(1)} collective-permute-done((f32[8,16,512]{2,1,0:T(8,128)S(1)}, f32[8,16,512]{2,1,0:T(8,128)S(1)}, u32[]{:S(2)}, u32[]{:S(2)}) %collective-permute-start) | collective-permute-done | bytes 262176 | tf_op jit(solution)/shard_map/while/body/eval_jaxpr/ppermute | solution.py:12
  113.7 2.5 broadcast.67.clone
  116.2 68.1 %while.145 = (s32[]{:T(128)}, f32[8,16,512]{2,1,0:T(8,128)S(1)}, f32[16,8,16,512]{3,2,0,1:T(8,128)}, s32[16]{0:T(128)S(1)}, f32[16,8]{1,0:T(8,128)S(1)}, /*index...) while((s32[]{:T(128)}, f32[8,16,512]{2,1,0:T(8,128)S(1)}, ...), condition=%wide.region_7.8_spmd, body=%wide.region_6.7_spmd.sunk | while | flops 458758 | bytes 1198375 | solution.py:88
  184.6 30.8 %while.152 = (s32[]{:T(128)}, f32[16,16,512]{2,1,0:T(8,128)S(1)}, s32[8]{0:T(128)S(1)}, f32[16,8]{0,1:T(8,128)S(1)}, f32[16,512]{1,0:T(8,128)S(1)}, /*index=5*/f...) while((s32[]{:T(128)}, f32[16,16,512]{2,1,0:T(8,128)S(1)}, ...), condition=%wide.region_9.10_spmd.clone, body=%wide.region_8.9_spmd.clone.sunk | while | flops 655367 | bytes 1704317 | solution.py:94
  215.4 23.4 %while.153 = (s32[]{:T(128)}, f32[16,16,512]{2,1,0:T(8,128)S(1)}, s32[8]{0:T(128)S(1)}, f32[16,8]{0,1:T(8,128)S(1)}, f32[16,512]{1,0:T(8,128)S(1)}, /*index=5*/f...) while((s32[]{:T(128)}, f32[16,16,512]{2,1,0:T(8,128)S(1)}, ...), condition=%wide.region_11.12_spmd.clone, body=%wide.region_10.11_spmd.clone.sunk | while | flops 786438 | bytes 1281393 | solution.py:51
  239.8 3.1 collective-permute-start.3
  242.9 1.3 collective-permute-start.2
  244.3 6.9 %collective-permute-done.3 = f32[16,16,512]{2,1,0:T(8,128)S(1)} collective-permute-done((f32[16,16,512]{2,1,0:T(8,128)S(1)}, f32[16,16,512]{2,1,0:T(8,128)S(1)}, u32[]{:S(2)}, u32[]{:S(2)}) %collective-permute-start.3) | collective-permute-done | bytes 524320 | tf_op jit(solution)/shard_map/while/body/eval_jaxpr/ppermute | solution.py:12
  251.2 28.8 %while.146 = (s32[]{:T(128)}, f32[16,16,512]{2,1,0:T(8,128)S(1)}, f32[8,16,16,512]{3,2,1,0:T(8,128)}, s32[8]{0:T(128)S(1)}, f32[16,8]{0,1:T(8,128)S(1)}, /*index...) while((s32[]{:T(128)}, f32[16,16,512]{2,1,0:T(8,128)S(1)}, ...), condition=%wide.region_13.14_spmd, body=%wide.region_12.13_spmd.sunk | while | flops 655365 | bytes 1806191 | solution.py:55
  280.0 5.0 copy.26
  285.0 58.9 %while.154 = (s32[]{:T(128)}, f32[8,16,512]{2,1,0:T(8,128)S(1)}, s32[16]{0:T(128)S(1)}, f32[16,8]{1,0:T(8,128)S(1)}, f32[16,512]{1,0:T(8,128)S(1)}, /*index=5*/f...) while((s32[]{:T(128)}, f32[8,16,512]{2,1,0:T(8,128)S(1)}, ...), condition=%wide.region_15.16_spmd.clone, body=%wide.region_14.15_spmd.clone.sunk | while | flops 327686 | bytes 868617 | solution.py:65
  343.9 26.2 %while.150 = (s32[]{:T(128)}, f32[8,16,512]{2,1,0:T(8,128)S(1)}, f32[8,16,512]{2,1,0:T(8,128)S(1)}, f32[16,512]{1,0:T(8,128)S(1)}, f32[8,512]{1,0:T(8,128)S(1)}, /*index=5*/s32[]{:T(128)}) while((s32[]{:T(128)}, f32[8,16,512]{2,1,0:T(8,128)S(1)}, f32[8,16,512]{2,1,0:T(8,128)S(1)}, f32[16,512]{1,0:T(8,128)S(1)}, ...), condition=%wide.region_17.18_spmd.clone, body=%wide.region_16.17_spmd.clone.sunk | while | flops 196610 | bytes 1884269 | solution.py:20
  344.0 3.5 collective-permute-start.1
  347.5 4.3 collective-permute-done.1
  351.9 4.4 collective-permute-start.1
  356.3 5.5 %collective-permute-done.1 = f32[8,16,512]{2,1,0:T(8,128)S(1)} collective-permute-done((f32[8,16,512]{2,1,0:T(8,128)S(1)}, f32[8,16,512]{2,1,0:T(8,128)S(1)}, u32[]{:S(2)}, u32[]{:S(2)}) %collective-permute-start.1) | collective-permute-done | bytes 262176 | tf_op jit(solution)/shard_map/while/body/eval_jaxpr/ppermute | solution.py:12
  361.9 4.4 collective-permute-start.1
  366.3 3.9 collective-permute-done.1
  370.2 83.3 %while.147 = (s32[]{:T(128)}, f32[8,16,512]{2,1,0:T(8,128)S(1)}, f32[16,8,16,512]{3,2,1,0:T(8,128)}, f32[16,8,16]{2,1,0:T(8,128)}, s32[16]{0:T(128)S(1)}, /*inde...) while((s32[]{:T(128)}, f32[8,16,512]{2,1,0:T(8,128)S(1)}, ...), condition=%wide.region_20.21_spmd, body=%wide.region_18.20_spmd.sunk | while | flops 393093 | bytes 1448215 | solution.py:74
  383.2 1.3 multiply_reduce_fusion.7
  388.4 1.3 multiply_reduce_fusion.7
  393.6 1.3 multiply_reduce_fusion.7
  454.9 75.8 %while.148 = (s32[]{:T(128)}, f32[16,16,512]{2,1,0:T(8,128)S(1)}, bf16[8,16,512]{2,1,0:T(8,128)(2,1)}, f32[8,16,512]{2,0,1:T(8,128)}, f32[8,16,16]{2,0,1:T(8,128...) while((s32[]{:T(128)}, f32[16,16,512]{2,1,0:T(8,128)S(1)}, ...), condition=%wide.region_25.26_spmd, body=%wide.region_21.25_spmd.sunk | while | flops 2522889 | bytes 7002969 | solution.py:118
  459.9 1.7 multiply_reduce_fusion.8
  461.7 1.8 dynamic_update_slice.71
  469.4 1.7 multiply_reduce_fusion.8
  471.1 1.8 dynamic_update_slice.71
  478.8 1.7 multiply_reduce_fusion.8
  480.6 1.8 dynamic_update_slice.71
  488.3 1.7 multiply_reduce_fusion.8
  490.1 1.8 dynamic_update_slice.71
  497.8 1.7 multiply_reduce_fusion.8
  499.6 1.8 dynamic_update_slice.71
  507.3 1.7 multiply_reduce_fusion.8
  509.0 1.8 dynamic_update_slice.71
  516.7 1.7 multiply_reduce_fusion.8
  518.5 1.8 dynamic_update_slice.71
  526.2 1.7 multiply_reduce_fusion.8
  528.0 1.8 dynamic_update_slice.71
  530.6 1.6 copy.52
  532.3 5.0 all-reduce
  (590 shorter events, 227.4 us)
Async XLA Ops:
  82.1 34.1 %copy-start.1 = (f32[16,8,512]{2,1,0:T(8,128)S(1)}, f32[16,8,512]{2,1,0:T(8,128)}, u32[]{:S(2)}) copy-start(f32[16,8,512]{2,1,0:T(8,128)} %get-tuple-element.2470) | copy-start | bytes 786436
  83.0 11.3 %collective-permute-start = (f32[8,16,512]{2,1,0:T(8,128)S(1)}, f32[8,16,512]{2,1,0:T(8,128)S(1)}, u32[]{:S(2)}, u32[]{:S(2)}) collective-permute-start(f32[8,16,512]{2,1,0:T(8,128)S(1)} %fusion.50), channel_id=1, source_target_pairs={{4,0},{8,4},{12,8},{5,1},{9,5},{13,9},{6,2},{10,6},{14,10},{7,3},{... | collective-permute-start | bytes 786440 | tf_op jit(solution)/shard_map/while/body/eval_jaxpr/ppermute | solution.py:12
  95.0 9.4 %collective-permute-start = (f32[8,16,512]{2,1,0:T(8,128)S(1)}, f32[8,16,512]{2,1,0:T(8,128)S(1)}, u32[]{:S(2)}, u32[]{:S(2)}) collective-permute-start(f32[8,16,512]{2,1,0:T(8,128)S(1)} %fusion.50), channel_id=1, source_target_pairs={{4,0},{8,4},{12,8},{5,1},{9,5},{13,9},{6,2},{10,6},{14,10},{7,3},{... | collective-permute-start | bytes 786440 | tf_op jit(solution)/shard_map/while/body/eval_jaxpr/ppermute | solution.py:12
  105.2 8.5 %collective-permute-start = (f32[8,16,512]{2,1,0:T(8,128)S(1)}, f32[8,16,512]{2,1,0:T(8,128)S(1)}, u32[]{:S(2)}, u32[]{:S(2)}) collective-permute-start(f32[8,16,512]{2,1,0:T(8,128)S(1)} %fusion.50), channel_id=1, source_target_pairs={{4,0},{8,4},{12,8},{5,1},{9,5},{13,9},{6,2},{10,6},{14,10},{7,3},{... | collective-permute-start | bytes 786440 | tf_op jit(solution)/shard_map/while/body/eval_jaxpr/ppermute | solution.py:12
  113.7 2.5 copy-start
  116.2 68.2 %copy-start.2 = (bf16[16,8,512]{2,1,0:T(8,128)(2,1)S(1)}, bf16[16,8,512]{2,1,0:T(8,128)(2,1)}, u32[]{:S(2)}) copy-start(bf16[16,8,512]{2,1,0:T(8,128)(2,1)} %param.28) | copy-start | bytes 393220
  184.6 30.8 %copy-start.3 = (f32[16,8,16]{2,1,0:T(8,128)S(1)}, f32[16,8,16]{2,1,0:T(8,128)}, u32[]{:S(2)}) copy-start(f32[16,8,16]{2,1,0:T(8,128)} %param.33) | copy-start | bytes 24580
  239.8 11.3 %collective-permute-start.3 = (f32[16,16,512]{2,1,0:T(8,128)S(1)}, f32[16,16,512]{2,1,0:T(8,128)S(1)}, u32[]{:S(2)}, u32[]{:S(2)}) collective-permute-start(f32[16,16,512]{2,1,0:T(8,128)S(1)} %get-tuple-element.1527), channel_id=1, source_target_pairs={{0,2},{1,3},{4,6},{5,7},{8,10},{9,11},{12,14},{13,15},{16,18},{17,... | collective-permute-start | bytes 1572872 | tf_op jit(solution)/shard_map/while/body/eval_jaxpr/ppermute | solution.py:12
  242.9 210.6 %collective-permute-start.2 = (f32[16,16,512]{2,1,0:T(8,128)}, f32[16,16,512]{2,1,0:T(8,128)S(1)}, u32[]{:S(2)}, u32[]{:S(2)}) collective-permute-start(f32[16,16,512]{2,1,0:T(8,128)} %get-tuple-element.1528), channel_id=1, source_target_pairs={{2,0},{3,1},{6,4},{7,5},{10,8},{11,9},{14,12},{15,13},{18,16},{19,... | collective-permute-start | bytes 1572872 | tf_op jit(solution)/shard_map/while/body/eval_jaxpr/ppermute | solution.py:12
  344.0 7.8 %collective-permute-start.1 = (f32[8,16,512]{2,1,0:T(8,128)S(1)}, f32[8,16,512]{2,1,0:T(8,128)S(1)}, u32[]{:S(2)}, u32[]{:S(2)}) collective-permute-start(f32[8,16,512]{2,1,0:T(8,128)S(1)} %fusion.51), channel_id=1, source_target_pairs={{0,4},{4,8},{8,12},{1,5},{5,9},{9,13},{2,6},{6,10},{10,14},{3,7},{... | collective-permute-start | bytes 786440 | tf_op jit(solution)/shard_map/while/body/eval_jaxpr/ppermute | solution.py:12
  351.9 9.9 %collective-permute-start.1 = (f32[8,16,512]{2,1,0:T(8,128)S(1)}, f32[8,16,512]{2,1,0:T(8,128)S(1)}, u32[]{:S(2)}, u32[]{:S(2)}) collective-permute-start(f32[8,16,512]{2,1,0:T(8,128)S(1)} %fusion.51), channel_id=1, source_target_pairs={{0,4},{4,8},{8,12},{1,5},{5,9},{9,13},{2,6},{6,10},{10,14},{3,7},{... | collective-permute-start | bytes 786440 | tf_op jit(solution)/shard_map/while/body/eval_jaxpr/ppermute | solution.py:12
  361.9 8.3 %collective-permute-start.1 = (f32[8,16,512]{2,1,0:T(8,128)S(1)}, f32[8,16,512]{2,1,0:T(8,128)S(1)}, u32[]{:S(2)}, u32[]{:S(2)}) collective-permute-start(f32[8,16,512]{2,1,0:T(8,128)S(1)} %fusion.51), channel_id=1, source_target_pairs={{0,4},{4,8},{8,12},{1,5},{5,9},{9,13},{2,6},{6,10},{10,14},{3,7},{... | collective-permute-start | bytes 786440 | tf_op jit(solution)/shard_map/while/body/eval_jaxpr/ppermute | solution.py:12
where the time goes:
time: 547 us; the launch traced here: 537 us
  loops' own time  197 us (36%)
  local copies, waits for them, and re-layouts  151 us (28%)
  other arithmetic  117 us (21%)
  waiting for transfers between devices  45.8 us (8%)
  starting transfers between devices  20.5 us (4%)
    ppermute x8, waiting for transfers between devices, shifted(): return lax.ppermute(block, axis, route)  45.8 us
    dynamic_slice x64, local copies, waits for them, and re-layouts, local(): col_offset, _ = lax.scan(col_forward_last, col_zero, jnp.arange(prows))  38.5 us
    mul x64, local copies, waits for them, and re-layouts, col_backward(): cot = output_map[i][:, :, None] * gyf[i][:, None, :] + carry  33.9 us
    another operation x1, loops' own time, local(): col_offset, _ = lax.scan(col_forward_last, col_zero, jnp.arange(prows))  31.7 us
    another operation x1, loops' own time, local(): lax.scan(col_backward, bottom_in, jnp.arange(prows), reverse=True)  31.6 us
    another operation x1, loops' own time, local(): _, (state, map_out) = lax.scan(col_forward_out, top_in, jnp.arange(prows))  31.4 us
    another operation x1, loops' own time, local(): lax.scan(col_backward_last, col_zero, jnp.arange(prows), reverse=True)  30.3 us
    another operation x1, loops' own time, local(): lax.scan(row_backward, right_in, jnp.arange(pcols), reverse=True)  26.6 us
  transfers between devices with their start and end apart: 8, of which 7 were waited for; matrix products, arithmetic and copies ran while one was open for 18% of the time, Pallas kernels for 0%

commit v1 on v0

v1 whole, which is shorter than its diff:
```python
import functools
import math
import jax
import jax.numpy as jnp
from jax import lax
from jax.experimental import pallas as pl
from jax.experimental.pallas import tpu as pltpu
from jax.sharding import PartitionSpec as P

CODES = 16
CHUNKS = 1
LOG2E = 1.4426950408889634
f32 = jnp.float32


def call(body, outs, scratch, name, args):
    vmem = pl.BlockSpec(memory_space=pltpu.VMEM)
    return pl.pallas_call(
        body,
        out_shape=tuple(outs),
        in_specs=[vmem] * len(args),
        out_specs=tuple([vmem] * len(outs)),
        scratch_shapes=scratch,
        name=name,
    )(*args)


def column_of(row, eye):
    return jnp.sum(jnp.where(eye, jnp.broadcast_to(row, eye.shape), 0.0), axis=1, keepdims=True)


def spread_map(map_ref, wide_ref):
    rows, cols, n = map_ref.shape
    turned = jnp.transpose(map_ref[...].reshape(rows * cols, n))
    for p in range(rows * cols):
        wide_ref[p] = jnp.broadcast_to(turned[:, p : p + 1], (n, 128))


def widen(tile, width):
    return jnp.concatenate([tile] * (width // 128), axis=1)


def prepare(steps_ref, patches_ref, codes_ref, mask_ref, log_ref, drive_ref, ms_ref, mx_ref, keep_ref):
    rows, cols, _ = steps_ref.shape
    maskf = mask_ref[...].astype(f32)
    keep = maskf * jnp.log(0.7 + 0.25 * codes_ref[...].astype(f32) / (CODES - 1))
    eye = lax.broadcasted_iota(jnp.int32, (cols, cols), 0) == lax.broadcasted_iota(jnp.int32, (cols, cols), 1)
    for i in range(rows):
        kept = column_of(keep[i : i + 1, :], eye)
        masked = column_of(maskf[i : i + 1, :], eye)
        step = steps_ref[i]
        x = patches_ref[i].astype(f32)
        masked_step = masked * step
        log_ref[i] = (kept * LOG2E) * step
        drive_ref[i] = masked_step * x
        ms_ref[i] = masked_step
        mx_ref[i] = masked * x
        keep_ref[i] = jnp.broadcast_to(kept, (cols, 128))


def row_ends(span, log_ref, drive_ref, rates_ref, in_ref, off_ref):
    rows, cols, _ = log_ref.shape
    lo, width = span
    lanes = pl.ds(lo, width)

    def one_row(i, _):
        rates = rates_ref[:, lanes]
        carry = None
        for j in range(cols):
            source = widen(in_ref[i * cols + j], width) * drive_ref[i, j : j + 1, lanes]
            if carry is None:
                carry = source
            else:
                carry = jnp.exp2(rates * log_ref[i, j : j + 1, lanes]) * carry + source
        off_ref[i] = carry
        return 0

    lax.fori_loop(0, rows, one_row, 0)


def first_rows(span, steps_ref, patches_ref, codes_ref, mask_ref, rates_ref, map_ref,
               off_ref, log_ref, drive_ref, ms_ref, mx_ref, keep_ref, in_ref):
    prepare(steps_ref, patches_ref, codes_ref, mask_ref, log_ref, drive_ref, ms_ref, mx_ref, keep_ref)
    spread_map(map_ref, in_ref)
    row_ends(span, log_ref, drive_ref, rates_ref, in_ref, off_ref)


def more_rows(span, log_ref, drive_ref, rates_ref, in_ref, off_ref):
    row_ends(span, log_ref, drive_ref, rates_ref, in_ref, off_ref)


def col_starts(span, log_ref, grad_ref, rates_ref, out_ref, off_ref, factor_ref):
    rows, cols, _ = log_ref.shape
    lo, width = span
    lanes = pl.ds(lo, width)
    for j in range(cols):
        off_ref[j] = jnp.zeros(off_ref.shape[1:], f32)

    def one_row(turn, _):
        i = rows - 1 - turn
        rates = rates_ref[:, lanes]
        for j in range(cols):
            cot = widen(out_ref[i * cols + j], width) * grad_ref[i, j : j + 1, lanes] + off_ref[j]
            off_ref[j] = jnp.exp2(rates * log_ref[i, j : j + 1, lanes]) * cot
        return 0

    lax.fori_loop(0, rows, one_row, 0)
    total = log_ref[0, :, lanes]
    for i in range(1, rows):
        total = total + log_ref[i, :, lanes]
    rates = rates_ref[:, lanes]
    for j in range(cols):
        factor_ref[j] = jnp.exp2(rates * total[j : j + 1])


def first_cols(span, log_ref, out_grad_ref, rates_ref, map_ref, off_ref, factor_ref, grad_ref, out_ref):
    for i in range(log_ref.shape[0]):
        grad_ref[i] = out_grad_ref[i].astype(f32)
    spread_map(map_ref, out_ref)
    col_starts(span, log_ref, grad_ref, rates_ref, out_ref, off_ref, factor_ref)


def more_cols(span, log_ref, grad_ref, rates_ref, out_ref, off_ref, factor_ref):
    col_starts(span, log_ref, grad_ref, rates_ref, out_ref, off_ref, factor_ref)


def forward(span, log_ref, drive_ref, rates_ref, in_ref, left_ref, row_ref, off_ref):
    rows, cols, _ = log_ref.shape
    lo, width = span
    lanes = pl.ds(lo, width)
    for j in range(cols):
        off_ref[j] = jnp.zeros(off_ref.shape[1:], f32)

    def one_row(i, _):
        rates = rates_ref[:, lanes]
        carry = left_ref[i]
        for j in range(cols):
            factor = jnp.exp2(rates * log_ref[i, j : j + 1, lanes])
            carry = factor * carry + widen(in_ref[i * cols + j], width) * drive_ref[i, j : j + 1, lanes]
            row_ref[i * cols + j] = carry
            off_ref[j] = factor * off_ref[j] + carry
        return 0

    lax.fori_loop(0, rows, one_row, 0)


def backward(span, log_ref, grad_ref, rates_ref, out_ref, bottom_ref, col_ref, off_ref, carry_ref):
    rows, cols, _ = log_ref.shape
    lo, width = span
    lanes = pl.ds(lo, width)
    for j in range(cols):
        carry_ref[j] = bottom_ref[j]

    def one_row(turn, _):
        i = rows - 1 - turn
        rates = rates_ref[:, lanes]
        lead = None
        for j in reversed(range(cols)):
            factor = jnp.exp2(rates * log_ref[i, j : j + 1, lanes])
            cot = widen(out_ref[i * cols + j], width) * grad_ref[i, j : j + 1, lanes] + carry_ref[j]
            col_ref[i * cols + j] = cot
            carry_ref[j] = factor * cot
            lead = factor * (cot if lead is None else cot + lead)
        off_ref[i] = lead
        return 0

    lax.fori_loop(0, rows, one_row, 0)


def finish(span, log_ref, drive_ref, grad_ref, rates_ref, in_ref, row_ref, col_ref, ms_ref, mx_ref, keep_ref,
           left_ref, top_ref, right_ref, *refs):
    chained = len(refs) == 9
    if chained:
        before_ref, gx_ref, gs_ref, maps_ref, carry_ref, drive_cot_ref, log_cot_ref = refs[0], *refs[3:]
    else:
        gx_ref, gs_ref, maps_ref, carry_ref, drive_cot_ref, log_cot_ref = refs
    rows, cols, _ = log_ref.shape
    n = rates_ref.shape[0]
    lo, width = span
    lanes = pl.ds(lo, width)
    for j in range(cols):
        carry_ref[j] = top_ref[j]
    spot = lax.broadcasted_iota(jnp.int32, (n, rows * cols), 1)

    def one_row(i, sums):
        map_in, map_out = sums
        rates = rates_ref[:, lanes]
        lead = right_ref[i]
        here = row_ref[i * cols + cols - 1]
        for j in reversed(range(cols)):
            p = i * cols + j
            left = row_ref[p - 1] if j > 0 else left_ref[i]
            factor = jnp.exp2(rates * log_ref[i, j : j + 1, lanes])
            above = carry_ref[j]
            state = factor * above + here
            carry_ref[j] = state
            col_cot = col_ref[p]
            row_cot = col_cot + lead
            lead = factor * row_cot
            log_cot = (col_cot * (factor * above) + lead * left) * rates
            drive_cot = row_cot * widen(in_ref[p], width)
            drive_cot_ref[j : j + 1, :] = jnp.sum(drive_cot, axis=0, keepdims=True)
            log_cot_ref[j : j + 1, :] = jnp.sum(log_cot, axis=0, keepdims=True)
            at = spot == p
            map_in = jnp.where(at, jnp.sum(row_cot * drive_ref[i, j : j + 1, lanes], axis=1, keepdims=True), map_in)
            map_out = jnp.where(at, jnp.sum(state * grad_ref[i, j : j + 1, lanes], axis=1, keepdims=True), map_out)
            here = left
        drive_cot = drive_cot_ref[...]
        gx_ref[i, :, lanes] = (drive_cot * ms_ref[i, :, lanes]).astype(jnp.bfloat16)
        gs_ref[i, :, lanes] = drive_cot * mx_ref[i, :, lanes] + log_cot_ref[...] * widen(keep_ref[i], width)
        return map_in, map_out

    zero = jnp.zeros((n, rows * cols), f32)
    start = (before_ref[0:n, :], before_ref[n:, :]) if chained else (zero, zero)
    map_in, map_out = lax.fori_loop(0, rows, one_row, start)
    maps_ref[0:n, :] = map_in
    maps_ref[n:, :] = map_out


def sd(*shape, dtype=f32):
    return jax.ShapeDtypeStruct(shape, dtype)


def relay(offset, factor, axis, forwards):
    size = lax.axis_size(axis)
    entering = None
    for turn in range(size - 1):
        route = [(turn, turn + 1)] if forwards else [(size - 1 - turn, size - 2 - turn)]
        sent = offset if entering is None else factor * entering + offset
        got = lax.ppermute(sent, axis, route)
        entering = got if entering is None else entering + got
    return jnp.zeros_like(offset) if entering is None else entering


def local(patches, steps, decay_codes, tissue_mask, decay_rates, input_map, output_map, out_grad):
    rows, cols, width = steps.shape
    n = decay_rates.shape[0]
    part = width // CHUNKS
    spans = [(k * part, part) for k in range(CHUNKS)]
    places = rows * cols
    field = sd(places, n, part)
    row_edge = sd(rows, n, part)
    col_edge = sd(cols, n, part)
    whole = sd(rows, cols, width)

    row_offs, col_offs, col_factors = [], [], []
    for k, span in enumerate(spans):
        tag = "_" + str(k)
        if k == 0:
            off, log, drive, ms, mx, keep, in_wide = call(
                functools.partial(first_rows, span),
                [row_edge, whole, whole, whole, whole, sd(rows, cols, 128), sd(places, n, 128)],
                [], "row_ends" + tag,
                (steps, patches, decay_codes, tissue_mask, decay_rates, input_map),
            )
        else:
            (off,) = call(functools.partial(more_rows, span), [row_edge], [], "row_ends" + tag,
                          (log, drive, decay_rates, in_wide))
        row_offs.append(off)
        if k == 0:
            off, factor, grad, out_wide = call(
                functools.partial(first_cols, span),
                [col_edge, col_edge, whole, sd(places, n, 128)],
                [], "col_starts" + tag,
                (log, out_grad, decay_rates, output_map),
            )
        else:
            off, factor = call(functools.partial(more_cols, span), [col_edge, col_edge], [], "col_starts" + tag,
                               (log, grad, decay_rates, out_wide))
        col_offs.append(off)
        col_factors.append(factor)

    many = lax.axis_size("cols") > 2
    row_total = jnp.sum(log, axis=1)
    lefts, tops, bottoms, rights, fields, cots = [], [], [], [], [], []
    for k, span in enumerate(spans):
        lo = span[0]
        row_factor = None
        if many:
            row_factor = jnp.exp2(row_total[:, None, lo : lo + part] * decay_rates[None, :, lo : lo + part])
        left = relay(row_offs[k], row_factor, "cols", True)
        bottom = relay(col_offs[k], col_factors[k], "rows", False)
        row_field, down = call(functools.partial(forward, span), [field, col_edge], [], "forward_" + str(k),
                               (log, drive, decay_rates, in_wide, left))
        top = relay(down, col_factors[k], "rows", True)
        col_field, lead = call(functools.partial(backward, span), [field, row_edge],
                               [pltpu.VMEM((cols, n, part), f32)], "backward_" + str(k),
                               (log, grad, decay_rates, out_wide, bottom))
        right = relay(lead, row_factor, "cols", False)
        lefts.append(left)
        tops.append(top)
        rights.append(right)
        fields.append(row_field)
        cots.append(col_field)

    maps = None
    for k, span in enumerate(spans):
        args = [log, drive, grad, decay_rates, in_wide, fields[k], cots[k], ms, mx, keep, lefts[k], tops[k], rights[k]]
        aliases = {}
        if maps is not None:
            args += [maps, gx, gs]
            aliases = {len(args) - 2: 0, len(args) - 1: 1}
        vmem = pl.BlockSpec(memory_space=pltpu.VMEM)
        gx, gs, maps = pl.pallas_call(
            functools.partial(finish, span),
            out_shape=(sd(rows, cols, width, dtype=jnp.bfloat16), whole, sd(2 * n, places)),
            in_specs=[vmem] * len(args),
            out_specs=(vmem, vmem, vmem),
            scratch_shapes=[pltpu.VMEM((cols, n, part), f32), pltpu.VMEM((cols, part), f32), pltpu.VMEM((cols, part), f32)],
            input_output_aliases=aliases,
            name="finish_" + str(k),
        )(*args)

    if lax.axis_size("chan") == 2:
        maps = maps + lax.ppermute(maps, "chan", [(0, 1), (1, 0)])
    else:
        maps = lax.psum(maps, "chan")
    turned = jnp.transpose(maps).reshape(rows, cols, 2 * n)
    return gx, gs, turned[:, :, :n], turned[:, :, n:]


def solution(mesh):
    in_specs = (
        P(("groups", "rows"), "cols", "chan"),
        P(("groups", "rows"), "cols", "chan"),
        P(("groups", "rows"), "cols"),
        P(("groups", "rows"), "cols"),
        P(None, "chan"),
        P(("groups", "rows"), "cols", None),
        P(("groups", "rows"), "cols", None),
        P(("groups", "rows"), "cols", "chan"),
    )
    out_specs = (
        P(("groups", "rows"), "cols", "chan"),
        P(("groups", "rows"), "cols", "chan"),
        P(("groups", "rows"), "cols", None),
        P(("groups", "rows"), "cols", None),
    )
    return jax.shard_map(local, mesh=mesh, in_specs=in_specs, out_specs=out_specs, check_vma=False)
```

time: 547 us -> 89 us (0.16); the launches traced: 537 us -> 88.6 us
  loops' own time: 197 us -> 0 us
  local copies, waits for them, and re-layouts: 151 us -> 5.13 us
  other arithmetic: 117 us -> 4.72 us
  Pallas kernels: 0 us -> 26.6 us
  waiting for transfers between devices: 45.8 us -> 37.7 us
  starting transfers between devices: 20.5 us -> 13.6 us
    another operation x10 -> x0, loops' own time: 197 us -> none  [the longest x1 31.7 us: local(): col_offset, _ = lax.scan(col_forward_last, col_zero, jnp.arange(prows))]
    dynamic_slice x112 -> x0, local copies, waits for them, and re-layouts: 66.1 us -> none  [the longest x64 38.5 us: local(): col_offset, _ = lax.scan(col_forward_last, col_zero, jnp.arange(prows))]
    dynamic_update_slice x56 -> x0, local copies, waits for them, and re-layouts: 36.3 us -> none  [the longest x32 21.6 us: local(): _, (state, map_out) = lax.scan(col_forward_out, top_in, jnp.arange(prows))]
    mul x248 -> x0, local copies, waits for them, and re-layouts: 35.7 us -> none  [the longest x64 33.9 us: col_backward(): cot = output_map[i][:, :, None] * gyf[i][:, None, :] + carry]
    reduce_sum x25 -> x0, other arithmetic: 34.9 us -> none  [the longest x16 20.6 us: col_forward_out(): return (carry, (carry, jnp.sum(gyf[i][:, None, :] * carry, axis=2)))]
    mul x50 -> x0, other arithmetic: 29 us -> none  [the longest x32 17.5 us: col_backward(): return (factor * cot, cot)]
    dynamic_update_slice x32 -> x0, other arithmetic: 27.8 us -> none  [the longest x16 12.7 us: local(): _, (state, map_out) = lax.scan(col_forward_out, top_in, jnp.arange(prows))]
    pallas_call x0 -> x5, Pallas kernels: none -> 26.6 us  [the longest x4 17.1 us: call(): pl.pallas_call(body, out_shape=tuple(outs), in_specs=[vmem] * len(args),...]
  transfers between devices with their start and end apart: 8 -> 9, of which waited for: 7 -> 5; matrix products, arithmetic and copies ran while one was open for 18% -> 1% of each run, Pallas kernels for 0% -> 9%
where the time goes in v1:
time: 89 us; the launch traced here: 88.6 us
  waiting for transfers between devices  37.7 us (42%)
  Pallas kernels  26.6 us (30%)
  starting transfers between devices  13.6 us (15%)
  local copies, waits for them, and re-layouts  5.13 us (6%)
  other arithmetic  4.72 us (5%)
    ppermute x8, waiting for transfers between devices, relay(): got = lax.ppermute(sent, axis, route)  36.3 us
    pallas_call x4, Pallas kernels, call(): pl.pallas_call(body, out_shape=tuple(outs), in_specs=[vmem] * len(args),...  17.1 us
    ppermute x8, starting transfers between devices, relay(): got = lax.ppermute(sent, axis, route)  13.6 us
    pallas_call x1, Pallas kernels, local(): pl.pallas_call(functools.partial(finish, span), out_shape=(sd(rows, cols,...  9.46 us
    unnamed x6, local copies, waits for them, and re-layouts  4.31 us
    add x2, other arithmetic, relay(): sent = offset if entering is None else factor * entering + offset  2.53 us
  transfers between devices with their start and end apart: 9, of which 5 were waited for; matrix products, arithmetic and copies ran while one was open for 1% of the time, Pallas kernels for 9%

profile of v1, /device:TPU:0, one launch (start us, length us, event | category | flops | bytes accessed | tf_op | source)
XLA Modules:
  0.0 88.6 jit_solution(14542284975489962217)
XLA Ops:
  0.6 1.4 %copy.16.codes_ref = s32[16,8]{1,0:T(8,128)} copy(s32[16,8]{0,1:T(8,128)} %param.10) | data formatting | bytes 1024 | tf_op args[2]
  2.0 1.4 %copy.17.mask_ref = s32[16,8]{1,0:T(8,128)} copy(s32[16,8]{0,1:T(8,128)} %param.11) | data formatting | bytes 1024 | tf_op args[3]
  3.3 4.1 %row_ends_0.1 = (f32[16,16,512]{2,1,0:T(8,128)}, f32[16,8,512]{2,1,0:T(8,128)}, f32[16,8,512]{2,1,0:T(8,128)}, f32[16,8,512]{2,1,0:T(8,128)}, f32[16,8,512]{2,1,...) custom-call(f32[16,8,512]{2,1,0:T(8,128)} %steps_ref.1, bf16[16,8,512]{2,1,0:T(8,128)(2,1)} %patches_ref.1, ...), custom_call_target="tpu_custom_call" | custom-call | tf_op jit(solution)/shard_map/row_ends_0/pallas_call | solution.py:18
  7.4 4.9 %collective-permute-start = (f32[16,16,512]{2,1,0:T(8,128)}, f32[16,16,512]{2,1,0:T(8,128)S(1)}, u32[]{:S(2)}, u32[]{:S(2)}) collective-permute-start(f32[16,16,512]{2,1,0:T(8,128)} %get-tuple-element.26), channel_id=1, source_target_pairs={{0,2},{1,3},{4,6},{5,7},{8,10},{9,11},{12,14},{13,15},{16,18},{17,... | collective-permute-start | bytes 1572872 | tf_op jit(solution)/shard_map/ppermute | solution.py:230
  12.3 3.6 %col_starts_0.1 = (f32[8,16,512]{2,1,0:T(8,128)}, f32[8,16,512]{2,1,0:T(8,128)}, f32[16,8,512]{2,1,0:T(8,128)}, f32[128,16,128]{2,1,0:T(8,128)}) custom-call(f32[16,8,512]{2,1,0:T(8,128)} %get-tuple-element.22.log_ref, bf16[16,8,512]{2,1,0:T(8,128)(2,1)} %out_grad_ref.1, f32[16,512]{1,0:T(8,128)} %rates_ref.9, f32[16,8,16]{2,1,0:T(8,128)} %map_ref.3), custom_call_target="tpu_custom_call" | custom-call | tf_op jit(solution)/shard_map/col_starts_0/pallas_call | solution.py:18
  15.9 0.7 collective-permute-start.1
  16.6 7.1 %collective-permute-done.left_ref = f32[16,16,512]{2,1,0:T(8,128)S(1)} collective-permute-done((f32[16,16,512]{2,1,0:T(8,128)}, f32[16,16,512]{2,1,0:T(8,128)S(1)}, u32[]{:S(2)}, u32[]{:S(2)}) %collective-permute-start) | collective-permute-done | bytes 524320 | tf_op jit(solution)/shard_map/ppermute | solution.py:230
  23.8 0.0 copy-start
  23.8 0.8 copy-done
  24.5 4.7 %forward_0.1 = (f32[128,16,512]{2,1,0:T(8,128)}, f32[8,16,512]{2,1,0:T(8,128)}) custom-call(f32[16,8,512]{2,1,0:T(8,128)} %get-tuple-element.22.log_ref, f32[16,8,512]{2,1,0:T(8,128)} %get-tuple-element.23.drive_ref, f32[16,512]{1,0:T(8,128)} %rates_ref.9, f32[128,16,128]{2,1,0:T(8,128)} %get-tuple-element.25.in_ref, f32[16,16,512]{2,1,0:T(8,128)} %copy-done), custom_call_target="tpu_custom_call" | custom-call | tf_op jit(solution)/shard_map/forward_0/pallas_call | solution.py:18
  29.3 3.5 %collective-permute-start.4 = (f32[8,16,512]{2,1,0:T(8,128)}, f32[8,16,512]{2,1,0:T(8,128)S(1)}, u32[]{:S(2)}, u32[]{:S(2)}) collective-permute-start(f32[8,16,512]{2,1,0:T(8,128)} %get-tuple-element.35), channel_id=1, source_target_pairs={{0,4},{1,5},{2,6},{3,7},{16,20},{17,21},{18,22},{19,23}} | collective-permute-start | bytes 786440 | tf_op jit(solution)/shard_map/ppermute | solution.py:230
  32.8 0.0 collective-permute-done.1
  32.8 5.0 %collective-permute-done.4 = f32[8,16,512]{2,1,0:T(8,128)S(1)} collective-permute-done((f32[8,16,512]{2,1,0:T(8,128)}, f32[8,16,512]{2,1,0:T(8,128)S(1)}, u32[]{:S(2)}, u32[]{:S(2)}) %collective-permute-start.4) | collective-permute-done | bytes 262176 | tf_op jit(solution)/shard_map/ppermute | solution.py:230
  37.7 1.2 %multiply_add_fusion.1 = (f32[8,16,512]{2,1,0:T(8,128)S(1)}, f32[8,16,512]{2,1,0:T(8,128)S(1)}) fusion(f32[8,16,512]{2,1,0:T(8,128)} %get-tuple-element.35, f32[8,16,512]{2,1,0:T(8,128)} %get-tuple-element.30, f32[8,16,512]{2,1,0:T(8,128)S(1)} %collective-permute-done.4, f32[8,16,512]{2,1,0:T(8,128)} %get-tuple-element.29, ...), kind=kLoop, calls=%fused_computation.1 | loop fusion | flops 262144 | bytes 1835008 | tf_op jit(solution)/shard_map/add | solution.py:229
  39.0 0.7 collective-permute-start.5
  39.7 0.7 collective-permute-start.2
  40.3 0.0 collective-permute-done.5
  40.4 0.0 collective-permute-done.2
  40.4 1.3 %multiply_add_fusion = (f32[8,16,512]{2,1,0:T(8,128)S(1)}, f32[8,16,512]{2,1,0:T(8,128)S(1)}, f32[8,16,512]{2,1,0:T(8,128)S(1)}, f32[8,16,512]{2,1,0:T(8,128)S(1)}) fusion(f32[8,16,512]{2,1,0:T(8,128)} %get-tuple-element.35, f32[8,16,512]{2,1,0:T(8,128)} %get-tuple-element.30, f32[8,16,512]{2,1,0:T(8,128)S(1)} %collective-permute-done.4, ...), kind=kLoop, calls=%fused_computation | loop fusion | flops 393216 | bytes 2883584 | tf_op jit(solution)/shard_map/add | solution.py:229
  41.7 1.3 %collective-permute-start.3 = (f32[8,16,512]{2,1,0:T(8,128)S(1)}, f32[8,16,512]{2,1,0:T(8,128)S(1)}, u32[]{:S(2)}, u32[]{:S(2)}) collective-permute-start(f32[8,16,512]{2,1,0:T(8,128)S(1)} %get-tuple-element.44), channel_id=1, source_target_pairs={{4,0},{5,1},{6,2},{7,3},{20,16},{21,17},{22,18},{23,19}} | collective-permute-start | bytes 786440 | tf_op jit(solution)/shard_map/ppermute | solution.py:230
  43.0 14.9 %collective-permute-done.3 = f32[8,16,512]{2,1,0:T(8,128)S(1)} collective-permute-done((f32[8,16,512]{2,1,0:T(8,128)S(1)}, f32[8,16,512]{2,1,0:T(8,128)S(1)}, u32[]{:S(2)}, u32[]{:S(2)}) %collective-permute-start.3) | collective-permute-done | bytes 262176 | tf_op jit(solution)/shard_map/ppermute | solution.py:230
  57.9 0.7 add.30.bottom_ref
  58.6 4.7 %backward_0.1 = (f32[128,16,512]{2,1,0:T(8,128)}, f32[16,16,512]{2,1,0:T(8,128)}) custom-call(f32[16,8,512]{2,1,0:T(8,128)} %get-tuple-element.22.log_ref, f32[16,8,512]{2,1,0:T(8,128)} %get-tuple-element.24.grad_ref, f32[16,512]{1,0:T(8,128)} %rates_ref.9, f32[128,16,128]{2,1,0:T(8,128)} %get-tuple-element.28.out_ref, f32[8,16,512]{2,1,0:T(8,128)} %add.30.bottom_ref), custom_call_target="tpu_custom_call" | custom-call | tf_op jit(solution)/shard_map/backward_0/pallas_call | solution.py:18
  63.3 1.3 %collective-permute-start.7 = (f32[16,16,512]{2,1,0:T(8,128)}, f32[16,16,512]{2,1,0:T(8,128)S(1)}, u32[]{:S(2)}, u32[]{:S(2)}) collective-permute-start(f32[16,16,512]{2,1,0:T(8,128)} %get-tuple-element.36), channel_id=1, source_target_pairs={{2,0},{3,1},{6,4},{7,5},{10,8},{11,9},{14,12},{15,13},{18,16},{19,... | collective-permute-start | bytes 1572872 | tf_op jit(solution)/shard_map/ppermute | solution.py:230
  64.6 0.7 collective-permute-start.6
  65.3 0.0 collective-permute-done.6
  65.3 0.7 add.34.top_ref
  66.0 9.3 %collective-permute-done.7.right_ref = f32[16,16,512]{2,1,0:T(8,128)S(1)} collective-permute-done((f32[16,16,512]{2,1,0:T(8,128)}, f32[16,16,512]{2,1,0:T(8,128)S(1)}, u32[]{:S(2)}, u32[]{:S(2)}) %collective-permute-start.7) | collective-permute-done | bytes 524320 | tf_op jit(solution)/shard_map/ppermute | solution.py:230
  75.3 0.0 copy-start.1
  75.3 0.8 copy-done.1
  76.2 9.5 %finish_0.1 = (bf16[16,8,512]{2,1,0:T(8,128)(2,1)}, f32[16,8,512]{2,1,0:T(8,128)}, f32[32,128]{1,0:T(8,128)}) custom-call(f32[16,8,512]{2,1,0:T(8,128)} %get-tuple-element.22.log_ref, f32[16,8,512]{2,1,0:T(8,128)} %get-tuple-element.23.drive_ref, f32[16,8,512]{2,1,0:T(8,128)} %get-tuple-element.24.grad_ref, f32[16,512]{1,0:T(8,128)} %rates_ref.9, ...), custom_call_target="tpu_custom_call" | custom-call | tf_op jit(solution)/shard_map/finish_0/pallas_call | solution.py:304
  85.6 0.0 collective-permute-start.8
  85.6 1.4 %collective-permute-done.8 = f32[32,128]{1,0:T(8,128)S(1)} collective-permute-done((f32[32,128]{1,0:T(8,128)}, f32[32,128]{1,0:T(8,128)S(1)}, u32[]{:S(2)}, u32[]{:S(2)}) %collective-permute-start.8) | collective-permute-done | bytes 16416 | tf_op jit(solution)/shard_map/ppermute | solution.py:315
  87.0 0.7 add_bitcast_fusion
  87.7 0.1 copy.18
  87.8 0.7 fusion
Async XLA Ops:
  7.4 16.3 %collective-permute-start = (f32[16,16,512]{2,1,0:T(8,128)}, f32[16,16,512]{2,1,0:T(8,128)S(1)}, u32[]{:S(2)}, u32[]{:S(2)}) collective-permute-start(f32[16,16,512]{2,1,0:T(8,128)} %get-tuple-element.26), channel_id=1, source_target_pairs={{0,2},{1,3},{4,6},{5,7},{8,10},{9,11},{12,14},{13,15},{16,18},{17,... | collective-permute-start | bytes 1572872 | tf_op jit(solution)/shard_map/ppermute | solution.py:230
  15.9 16.8 %collective-permute-start.1 = (f32[8,16,512]{2,1,0:T(8,128)}, f32[8,16,512]{2,1,0:T(8,128)S(1)}, u32[]{:S(2)}, u32[]{:S(2)}) collective-permute-start(f32[8,16,512]{2,1,0:T(8,128)} %get-tuple-element.29), channel_id=1, source_target_pairs={{12,8},{13,9},{14,10},{15,11},{28,24},{29,25},{30,26},{31,27}} | collective-permute-start | bytes 786440 | tf_op jit(solution)/shard_map/ppermute | solution.py:230
  23.8 0.8 copy-start
  29.3 8.5 %collective-permute-start.4 = (f32[8,16,512]{2,1,0:T(8,128)}, f32[8,16,512]{2,1,0:T(8,128)S(1)}, u32[]{:S(2)}, u32[]{:S(2)}) collective-permute-start(f32[8,16,512]{2,1,0:T(8,128)} %get-tuple-element.35), channel_id=1, source_target_pairs={{0,4},{1,5},{2,6},{3,7},{16,20},{17,21},{18,22},{19,23}} | collective-permute-start | bytes 786440 | tf_op jit(solution)/shard_map/ppermute | solution.py:230
  39.0 1.4 %collective-permute-start.5 = (f32[8,16,512]{2,1,0:T(8,128)S(1)}, f32[8,16,512]{2,1,0:T(8,128)S(1)}, u32[]{:S(2)}, u32[]{:S(2)}) collective-permute-start(f32[8,16,512]{2,1,0:T(8,128)S(1)} %get-tuple-element.46), channel_id=1, source_target_pairs={{4,8},{5,9},{6,10},{7,11},{20,24},{21,25},{22,26},{23,27}} | collective-permute-start | bytes 786440 | tf_op jit(solution)/shard_map/ppermute | solution.py:230
  39.7 0.7 collective-permute-start.2
  41.7 16.2 %collective-permute-start.3 = (f32[8,16,512]{2,1,0:T(8,128)S(1)}, f32[8,16,512]{2,1,0:T(8,128)S(1)}, u32[]{:S(2)}, u32[]{:S(2)}) collective-permute-start(f32[8,16,512]{2,1,0:T(8,128)S(1)} %get-tuple-element.44), channel_id=1, source_target_pairs={{4,0},{5,1},{6,2},{7,3},{20,16},{21,17},{22,18},{23,19}} | collective-permute-start | bytes 786440 | tf_op jit(solution)/shard_map/ppermute | solution.py:230
  63.3 12.0 %collective-permute-start.7 = (f32[16,16,512]{2,1,0:T(8,128)}, f32[16,16,512]{2,1,0:T(8,128)S(1)}, u32[]{:S(2)}, u32[]{:S(2)}) collective-permute-start(f32[16,16,512]{2,1,0:T(8,128)} %get-tuple-element.36), channel_id=1, source_target_pairs={{2,0},{3,1},{6,4},{7,5},{10,8},{11,9},{14,12},{15,13},{18,16},{19,... | collective-permute-start | bytes 1572872 | tf_op jit(solution)/shard_map/ppermute | solution.py:230
  64.6 0.7 collective-permute-start.6
  75.3 0.8 copy-start.1
  85.6 1.4 %collective-permute-start.8 = (f32[32,128]{1,0:T(8,128)}, f32[32,128]{1,0:T(8,128)S(1)}, u32[]{:S(2)}, u32[]{:S(2)}) collective-permute-start(f32[32,128]{1,0:T(8,128)} %get-tuple-element.39), channel_id=1, source_target_pairs={{0,1},{1,0},{2,3},{3,2},{4,5},{5,4},{6,7},{7,6},{8,9},{9,8},{10,11... | collective-permute-start | bytes 49160 | tf_op jit(solution)/shard_map/ppermute | solution.py:315
